TPU v7x, 32 devices: a whole 2x2x4 slice. The times are simulated.
32 devices in a mesh: seq: 4 (over y, core), ctx: 8 (over z, x).
Axes of the slice: x: 2, y: 2, z: 4, core: 2. Of those that a mesh axis runs over, the one named last changes fastest.
Arguments:
- tokens: bfloat16 [4, 2048, 1152], P('seq', 'ctx'), may hold values from -6 to 6
- prefix: int32 [4], P('seq'), may hold values from 204 to 1024
- gain_one: bfloat16 [1152], P('seq'), may hold values from 0.5 to 1.5
- w_query: bfloat16 [1152, 1152], P('seq', 'ctx'), may hold values from -0.1875 to 0.1875
- w_key: bfloat16 [1152, 384], P('seq', 'ctx'), may hold values from -0.1875 to 0.1875
- value_weight: bfloat16 [1152, 384], P('seq', 'ctx'), may hold values from -0.1875 to 0.1875
- w_out: bfloat16 [1152, 1152], P('seq', 'ctx'), may hold values from -6 to 6
- gain_two: bfloat16 [1152], P('seq'), may hold values from 0.5 to 1.5
- w_gate: bfloat16 [1152, 3072], P('seq', 'ctx'), may hold values from -0.1875 to 0.1875
- w_up: bfloat16 [1152, 3072], P('seq', 'ctx'), may hold values from -0.1875 to 0.1875
- w_down: bfloat16 [3072, 1152], P('seq', 'ctx'), may hold values from -0.109375 to 0.109375
- cotangent: bfloat16 [4, 2048, 1152], P('seq', 'ctx'), may hold values from -6 to 6
Outputs:
- output: bfloat16 [4, 2048, 1152], P('seq', 'ctx')
- input_grad: float32 [4, 2048, 1152], P('seq', 'ctx')
- first_gain_gradient: float32 [1152], P('seq')
- grad_query: float32 [1152, 1152], P('seq', 'ctx')
- grad_key: float32 [1152, 384], P('seq', 'ctx')
- grad_value: float32 [1152, 384], P('seq', 'ctx')
- grad_out: float32 [1152, 1152], P('seq', 'ctx')
- second_gain_gradient: float32 [1152], P('seq')
- grad_gate: float32 [1152, 3072], P('seq', 'ctx')
- grad_up: float32 [1152, 3072], P('seq', 'ctx')
- grad_down: float32 [3072, 1152], P('seq', 'ctx')
All inputs are finite; a program needn't handle non-finite values.
Results may differ from a plain program's by a relative error of at most 0.022.
Values may be sent and summed in bfloat16 or wider, within the bound.
A program may use at most 192 MiB of HBM per device.

v0:
```python
import functools

import jax
import jax.numpy as jnp
from jax import lax
from jax.experimental import pallas as pl
from jax.experimental.pallas import tpu as pltpu
from jax.sharding import PartitionSpec as P

QUERY_HEADS = 18
KEY_VALUE_HEADS = 6
HEAD_SIZE = 64


EPSILON = 1e-05
ROTARY_BASE = 10000.0

LANES = 128
Z_SIZE = 4
VMEM_LIMIT = 66_000_000
PLANE_LANES = 640
F32 = jnp.float32
BF16 = jnp.bfloat16
NT = (((1,), (1,)), ((), ()))


def rotary_tables(positions, head_width):
    half_width = head_width // 2
    frequency = ROTARY_BASE ** (-jnp.arange(half_width, dtype=jnp.float32) * 2.0 / head_width)
    angles = positions.astype(jnp.float32)[:, None] * frequency[None, :]
    return (jnp.cos(angles)[:, None, :], jnp.sin(angles)[:, None, :])


def apply_rotation(values_in, cosine_table, sine_values):
    half_width = values_in.shape[-1] // 2
    first = values_in[..., :half_width]
    second = values_in[..., half_width:]
    return jnp.concatenate(
        [first * cosine_table - second * sine_values, second * cosine_table + first * sine_values],
        axis=-1,
    )


def inverse_rotation(grads_in, cosine_table, sine_values):
    half_width = grads_in.shape[-1] // 2
    first = grads_in[..., :half_width]
    second = grads_in[..., half_width:]
    return jnp.concatenate(
        [first * cosine_table + second * sine_values, second * cosine_table - first * sine_values],
        axis=-1,
    )


def gather_weights(w_query, w_key, value_weight, w_out, w_gate, w_up, w_down, gain_one, gain_two):
    columns = (
        lax.all_gather(w_query, "ctx", axis=1, tiled=True),
        lax.all_gather(w_key, "ctx", axis=1, tiled=True),
        lax.all_gather(value_weight, "ctx", axis=1, tiled=True),
        lax.all_gather(w_out, "ctx", axis=1, tiled=True),
        lax.all_gather(w_gate, "ctx", axis=1, tiled=True),
        lax.all_gather(w_up, "ctx", axis=1, tiled=True),
        lax.all_gather(w_down, "ctx", axis=1, tiled=True),
    )
    return (
        lax.all_gather(columns[0], "seq", axis=0, tiled=True),
        lax.all_gather(columns[1], "seq", axis=0, tiled=True),
        lax.all_gather(columns[2], "seq", axis=0, tiled=True),
        lax.all_gather(columns[3], "seq", axis=0, tiled=True),
        lax.all_gather(columns[4], "seq", axis=0, tiled=True),
        lax.all_gather(columns[5], "seq", axis=0, tiled=True),
        lax.all_gather(columns[6], "seq", axis=0, tiled=True),
        lax.all_gather(gain_one, "seq", axis=0, tiled=True),
        lax.all_gather(gain_two, "seq", axis=0, tiled=True),
    )


def gather_pairs(key_rotated, value_reduced):
    return (
        lax.all_gather(key_rotated, "ctx", axis=1, tiled=True),
        lax.all_gather(value_reduced, "ctx", axis=1, tiled=True),
    )


def head_major(whole_result, sequence_count):
    sequence_length = whole_result.shape[1]
    return (
        whole_result.reshape(sequence_count, sequence_length, KEY_VALUE_HEADS, HEAD_SIZE)
        .transpose(0, 2, 1, 3)
        .reshape(sequence_count * KEY_VALUE_HEADS, sequence_length, HEAD_SIZE)
    )


def per_device(
    tokens,
    prefix,
    gain_one,
    w_query,
    w_key,
    value_weight,
    w_out,
    gain_two,
    w_gate,
    w_up,
    w_down,
    cotangent,
):
    sequence_count, token_local, model_width = tokens.shape
    sequence_length = token_local * lax.axis_size("ctx")
    number_of_rows = sequence_count * token_local
    queries_per_key_head = QUERY_HEADS // KEY_VALUE_HEADS
    score_scale = HEAD_SIZE ** (-0.5)
    gathered = gather_weights(
        w_query, w_key, value_weight, w_out, w_gate, w_up, w_down, gain_one, gain_two
    )
    full_query, full_key, full_value, full_out, full_gate, full_up, full_down = gathered[:7]
    first_norm = gathered[7].astype(jnp.float32)
    second_norm = gathered[8].astype(jnp.float32)
    input_rows = tokens.reshape(number_of_rows, model_width).astype(jnp.float32)
    first_factor = lax.rsqrt(jnp.mean(input_rows * input_rows, axis=-1, keepdims=True) + EPSILON)
    first_normalized_input = input_rows * first_factor
    normalized_rows = (first_normalized_input * first_norm).astype(jnp.bfloat16)
    query_pre = jnp.dot(normalized_rows, full_query, preferred_element_type=jnp.float32)
    key_prerotation = jnp.dot(normalized_rows, full_key, preferred_element_type=jnp.float32)
    value_reduced = jnp.dot(normalized_rows, full_value, preferred_element_type=jnp.float32).astype(
        jnp.bfloat16
    )
    positions = lax.axis_index("ctx") * token_local + jnp.arange(token_local, dtype=jnp.int32)
    cosine_table, sine_values = rotary_tables(positions, HEAD_SIZE)
    query_rows = apply_rotation(
        query_pre.reshape(sequence_count, token_local, QUERY_HEADS, HEAD_SIZE),
        cosine_table,
        sine_values,
    ).astype(jnp.bfloat16)
    key_rotated = apply_rotation(
        key_prerotation.reshape(sequence_count, token_local, KEY_VALUE_HEADS, HEAD_SIZE),
        cosine_table,
        sine_values,
    ).astype(jnp.bfloat16)
    key_rotated = key_rotated.reshape(sequence_count, token_local, KEY_VALUE_HEADS * HEAD_SIZE)
    value_reduced = value_reduced.reshape(sequence_count, token_local, KEY_VALUE_HEADS * HEAD_SIZE)
    keys_all, values_all = gather_pairs(key_rotated, value_reduced)
    query_block_list = query_rows.reshape(
        sequence_count, token_local, KEY_VALUE_HEADS, queries_per_key_head, HEAD_SIZE
    ).transpose(0, 2, 3, 1, 4)
    query_block_list = query_block_list.reshape(
        sequence_count * KEY_VALUE_HEADS, queries_per_key_head, token_local, HEAD_SIZE
    )
    key_blocks = head_major(keys_all, sequence_count)
    value_blocks = head_major(values_all, sequence_count)
    prefix_repeated = jnp.repeat(prefix, KEY_VALUE_HEADS)
    key_place = jnp.arange(sequence_length, dtype=jnp.int32)

    def visible_for(prefix_len):
        return (key_place[None, :] <= positions[:, None]) | (key_place[None, :] < prefix_len)

    def attend(block_item):
        query_block, key_block, value_block, prefix_len = block_item
        scores = (
            jnp.einsum("gqd,kd->gqk", query_block, key_block, preferred_element_type=jnp.float32)
            * score_scale
        )
        scores = jnp.where(visible_for(prefix_len)[None], scores, -1e30)
        row_max = jnp.max(scores, axis=-1, keepdims=True)
        expo = jnp.exp(scores - row_max)
        total = jnp.sum(expo, axis=-1, keepdims=True)
        probs_low = (expo / total).astype(jnp.bfloat16)
        result = jnp.einsum(
            "gqk,kd->gqd", probs_low, value_block, preferred_element_type=jnp.float32
        )
        return (result.astype(jnp.bfloat16), (row_max + jnp.log(total))[..., 0])

    attention_result_blocks, log_totals = lax.map(
        attend, (query_block_list, key_blocks, value_blocks, prefix_repeated)
    )
    attention_result = attention_result_blocks.reshape(
        sequence_count, KEY_VALUE_HEADS, queries_per_key_head, token_local, HEAD_SIZE
    ).transpose(0, 3, 1, 2, 4)
    attention_result = attention_result.reshape(number_of_rows, QUERY_HEADS * HEAD_SIZE)
    mixed_output = input_rows + jnp.dot(
        attention_result, full_out, preferred_element_type=jnp.float32
    )
    second_factor = lax.rsqrt(
        jnp.mean(mixed_output * mixed_output, axis=-1, keepdims=True) + EPSILON
    )
    second_normalized_input = mixed_output * second_factor
    normalized_second = (second_normalized_input * second_norm).astype(jnp.bfloat16)
    gate = jnp.dot(normalized_second, full_gate, preferred_element_type=jnp.float32)
    up_part = jnp.dot(normalized_second, full_up, preferred_element_type=jnp.float32)
    sigmoid_gate = jax.nn.sigmoid(gate)
    activated = gate * sigmoid_gate
    hidden = (activated * up_part).astype(jnp.bfloat16)
    result_rows = mixed_output + jnp.dot(hidden, full_down, preferred_element_type=jnp.float32)
    output = result_rows.astype(jnp.bfloat16).reshape(sequence_count, token_local, model_width)
    gathered = gather_weights(
        w_query, w_key, value_weight, w_out, w_gate, w_up, w_down, gain_one, gain_two
    )
    full_query, full_key, full_value, full_out, full_gate, full_up, full_down = gathered[:7]
    grad_rows_in = cotangent.reshape(number_of_rows, model_width)
    grad_down = jnp.dot(hidden.T, grad_rows_in, preferred_element_type=jnp.float32)
    dhidden = jnp.dot(grad_rows_in, full_down.T, preferred_element_type=jnp.float32)
    dgate = (dhidden * up_part * sigmoid_gate * (1.0 + gate * (1.0 - sigmoid_gate))).astype(
        jnp.bfloat16
    )
    dup_part = (dhidden * activated).astype(jnp.bfloat16)
    grad_gate = jnp.dot(normalized_second.T, dgate, preferred_element_type=jnp.float32)
    grad_up = jnp.dot(normalized_second.T, dup_part, preferred_element_type=jnp.float32)
    normalized_second_grad = jnp.dot(dgate, full_gate.T, preferred_element_type=jnp.float32)
    normalized_second_grad = normalized_second_grad + jnp.dot(
        dup_part, full_up.T, preferred_element_type=jnp.float32
    )
    second_gain_gradient = jnp.sum(normalized_second_grad * second_normalized_input, axis=0)
    second_scaled = normalized_second_grad * second_norm
    dmixed = grad_rows_in.astype(jnp.float32) + second_factor * (
        second_scaled
        - second_normalized_input
        * jnp.mean(second_scaled * second_normalized_input, axis=-1, keepdims=True)
    )
    dproj = dmixed.astype(jnp.bfloat16)
    grad_out = jnp.dot(attention_result.T, dproj, preferred_element_type=jnp.float32)
    attention_result_grad = jnp.dot(dproj, full_out.T, preferred_element_type=jnp.float32).astype(
        jnp.bfloat16
    )
    attention_result_block_grads = attention_result_grad.reshape(
        sequence_count, token_local, KEY_VALUE_HEADS, queries_per_key_head, HEAD_SIZE
    ).transpose(0, 2, 3, 1, 4)
    attention_result_block_grads = attention_result_block_grads.reshape(
        sequence_count * KEY_VALUE_HEADS, queries_per_key_head, token_local, HEAD_SIZE
    )
    keys_all, values_all = gather_pairs(key_rotated, value_reduced)
    key_blocks = head_major(keys_all, sequence_count)
    value_blocks = head_major(values_all, sequence_count)

    def attend_back(block_item):
        query_block, key_block, value_block, prefix_len, log_total, dout_block = block_item
        scores = (
            jnp.einsum("gqd,kd->gqk", query_block, key_block, preferred_element_type=jnp.float32)
            * score_scale
        )
        visible = visible_for(prefix_len)[None]
        probs = jnp.where(
            visible, jnp.exp(jnp.where(visible, scores, -1e30) - log_total[..., None]), 0.0
        )
        dvalues = jnp.einsum(
            "gqk,gqd->kd",
            probs.astype(jnp.bfloat16),
            dout_block,
            preferred_element_type=jnp.float32,
        )
        dprobs = jnp.einsum(
            "gqd,kd->gqk", dout_block, value_block, preferred_element_type=jnp.float32
        )
        dscores = (probs * (dprobs - jnp.sum(probs * dprobs, axis=-1, keepdims=True))).astype(
            jnp.bfloat16
        )
        dquery = (
            jnp.einsum("gqk,kd->gqd", dscores, key_block, preferred_element_type=jnp.float32)
            * score_scale
        )
        dkeys = (
            jnp.einsum("gqk,gqd->kd", dscores, query_block, preferred_element_type=jnp.float32)
            * score_scale
        )
        return (dquery, dkeys, dvalues)

    query_block_grads, key_block_grads, value_block_grads = lax.map(
        attend_back,
        (
            query_block_list,
            key_blocks,
            value_blocks,
            prefix_repeated,
            log_totals,
            attention_result_block_grads,
        ),
    )
    key_grads_combined = key_block_grads.reshape(
        sequence_count, KEY_VALUE_HEADS, sequence_length, HEAD_SIZE
    ).transpose(0, 2, 1, 3)
    key_grads_combined = key_grads_combined.reshape(
        sequence_count, sequence_length, KEY_VALUE_HEADS * HEAD_SIZE
    )
    value_grads_combined = value_block_grads.reshape(
        sequence_count, KEY_VALUE_HEADS, sequence_length, HEAD_SIZE
    ).transpose(0, 2, 1, 3)
    value_grads_combined = value_grads_combined.reshape(
        sequence_count, sequence_length, KEY_VALUE_HEADS * HEAD_SIZE
    )
    key_grads_local, value_grads_local = (
        lax.psum_scatter(
            key_grads_combined.astype(jnp.bfloat16), "ctx", scatter_dimension=1, tiled=True
        ).astype(jnp.float32),
        lax.psum_scatter(
            value_grads_combined.astype(jnp.bfloat16), "ctx", scatter_dimension=1, tiled=True
        ).astype(jnp.float32),
    )
    key_prerotation_grad = inverse_rotation(
        key_grads_local.reshape(sequence_count, token_local, KEY_VALUE_HEADS, HEAD_SIZE),
        cosine_table,
        sine_values,
    )
    key_prerotation_grad = key_prerotation_grad.astype(jnp.bfloat16).reshape(
        number_of_rows, KEY_VALUE_HEADS * HEAD_SIZE
    )
    value_reduced_grad = value_grads_local.astype(jnp.bfloat16).reshape(
        number_of_rows, KEY_VALUE_HEADS * HEAD_SIZE
    )
    query_row_grads = query_block_grads.reshape(
        sequence_count, KEY_VALUE_HEADS, queries_per_key_head, token_local, HEAD_SIZE
    ).transpose(0, 3, 1, 2, 4)
    query_row_grads = query_row_grads.reshape(sequence_count, token_local, QUERY_HEADS, HEAD_SIZE)
    dquery_pre = (
        inverse_rotation(query_row_grads, cosine_table, sine_values)
        .astype(jnp.bfloat16)
        .reshape(number_of_rows, QUERY_HEADS * HEAD_SIZE)
    )
    grad_query = jnp.dot(normalized_rows.T, dquery_pre, preferred_element_type=jnp.float32)
    grad_key = jnp.dot(normalized_rows.T, key_prerotation_grad, preferred_element_type=jnp.float32)
    grad_value = jnp.dot(normalized_rows.T, value_reduced_grad, preferred_element_type=jnp.float32)
    normalized_grad = jnp.dot(dquery_pre, full_query.T, preferred_element_type=jnp.float32)
    normalized_grad = normalized_grad + jnp.dot(
        key_prerotation_grad, full_key.T, preferred_element_type=jnp.float32
    )
    normalized_grad = normalized_grad + jnp.dot(
        value_reduced_grad, full_value.T, preferred_element_type=jnp.float32
    )
    first_gain_gradient = jnp.sum(normalized_grad * first_normalized_input, axis=0)
    first_scaled = normalized_grad * first_norm
    input_grad = dmixed + first_factor * (
        first_scaled
        - first_normalized_input
        * jnp.mean(first_scaled * first_normalized_input, axis=-1, keepdims=True)
    )
    input_grad = input_grad.reshape(sequence_count, token_local, model_width)
    partial_value = (
        lax.psum_scatter(
            grad_query.astype(jnp.bfloat16), "seq", scatter_dimension=0, tiled=True
        ).astype(jnp.float32),
        lax.psum_scatter(
            grad_key.astype(jnp.bfloat16), "seq", scatter_dimension=0, tiled=True
        ).astype(jnp.float32),
        lax.psum_scatter(
            grad_value.astype(jnp.bfloat16), "seq", scatter_dimension=0, tiled=True
        ).astype(jnp.float32),
        lax.psum_scatter(
            grad_out.astype(jnp.bfloat16), "seq", scatter_dimension=0, tiled=True
        ).astype(jnp.float32),
        lax.psum_scatter(
            grad_gate.astype(jnp.bfloat16), "seq", scatter_dimension=0, tiled=True
        ).astype(jnp.float32),
        lax.psum_scatter(
            grad_up.astype(jnp.bfloat16), "seq", scatter_dimension=0, tiled=True
        ).astype(jnp.float32),
        lax.psum_scatter(
            grad_down.astype(jnp.bfloat16), "seq", scatter_dimension=0, tiled=True
        ).astype(jnp.float32),
        lax.psum_scatter(
            first_gain_gradient.astype(jnp.bfloat16), "seq", scatter_dimension=0, tiled=True
        ).astype(jnp.float32),
        lax.psum_scatter(
            second_gain_gradient.astype(jnp.bfloat16), "seq", scatter_dimension=0, tiled=True
        ).astype(jnp.float32),
    )
    owned = (
        lax.psum_scatter(
            partial_value[0].astype(jnp.bfloat16), "ctx", scatter_dimension=1, tiled=True
        ).astype(jnp.float32),
        lax.psum_scatter(
            partial_value[1].astype(jnp.bfloat16), "ctx", scatter_dimension=1, tiled=True
        ).astype(jnp.float32),
        lax.psum_scatter(
            partial_value[2].astype(jnp.bfloat16), "ctx", scatter_dimension=1, tiled=True
        ).astype(jnp.float32),
        lax.psum_scatter(
            partial_value[3].astype(jnp.bfloat16), "ctx", scatter_dimension=1, tiled=True
        ).astype(jnp.float32),
        lax.psum_scatter(
            partial_value[4].astype(jnp.bfloat16), "ctx", scatter_dimension=1, tiled=True
        ).astype(jnp.float32),
        lax.psum_scatter(
            partial_value[5].astype(jnp.bfloat16), "ctx", scatter_dimension=1, tiled=True
        ).astype(jnp.float32),
        lax.psum_scatter(
            partial_value[6].astype(jnp.bfloat16), "ctx", scatter_dimension=1, tiled=True
        ).astype(jnp.float32),
    )
    gains_owned = lax.psum((partial_value[7], partial_value[8]), "ctx")
    final_grads = owned + gains_owned
    return (
        output,
        input_grad,
        final_grads[7],
        final_grads[0],
        final_grads[1],
        final_grads[2],
        final_grads[3],
        final_grads[8],
        final_grads[4],
        final_grads[5],
        final_grads[6],
    )


def my_place():
    seq_at, ctx_at = lax.axis_index("seq"), lax.axis_index("ctx")
    return ctx_at // 2, lax.rem(ctx_at, 2), seq_at // 2, lax.rem(seq_at, 2)


def flipped(at, flip):
    return 1 - at if flip else at


def lane_ids(rows):
    return lax.broadcasted_iota(jnp.int32, (rows, LANES), 1)


def rotate_halves(tile, cosine, sine):
    lower = lax.rem(lane_ids(tile.shape[0]), HEAD_SIZE) < HEAD_SIZE // 2
    swapped = jnp.where(
        lower, pltpu.roll(tile, LANES - HEAD_SIZE // 2, 1), pltpu.roll(tile, HEAD_SIZE // 2, 1)
    )
    return tile * cosine + swapped * sine


def pair_tiles(natural):
    lower = lane_ids(natural[0].shape[0]) < HEAD_SIZE
    tiles = []
    for pair in range(3):
        for member in range(3):
            one, two = 6 * pair + member, 6 * pair + 3 + member
            left, right = natural[one // 2], natural[two // 2]
            if one % 2:
                left, right = pltpu.roll(left, HEAD_SIZE, 1), pltpu.roll(right, HEAD_SIZE, 1)
            tiles.append(jnp.where(lower, left, right))
    return tiles


def natural_tiles(paired):
    lower = lane_ids(paired[0].shape[0]) < HEAD_SIZE
    tiles = []
    for at in range(9):
        sides = []
        for side in range(2):
            head = 2 * at + side
            tile = paired[head // 6 * 3 + head % 3]
            if (head % 6) // 3 != side:
                tile = pltpu.roll(tile, HEAD_SIZE, 1)
            sides.append(tile)
        tiles.append(jnp.where(lower, sides[0], sides[1]))
    return tiles


def normalized(rows):
    factor = lax.rsqrt(jnp.mean(rows * rows, axis=-1, keepdims=True) + EPSILON)
    return factor, rows * factor


def vmem_specs(count):
    return [pl.BlockSpec(memory_space=pltpu.VMEM)] * count


def any_specs(count):
    return [pl.BlockSpec(memory_space=pl.ANY)] * count


def cost(flops, moved, transcendentals=0):
    return pl.CostEstimate(flops=int(flops), bytes_accessed=int(moved), transcendentals=int(transcendentals))


def params():
    return pltpu.CompilerParams(vmem_limit_bytes=VMEM_LIMIT)


def masked_pair(block, half, other):
    inside = (lane_ids(block.shape[0]) < HEAD_SIZE) == (half == 0)
    return jnp.where(inside, block.astype(F32), other)


def core_rows(core):
    return pl.ds(pl.multiple_of(core * 256, 256), 256)


def turned_blocks(matrix, parts):
    flat = matrix.astype(F32).T.astype(BF16)
    return flat.reshape(parts, flat.shape[0] // parts, flat.shape[1])


class Gathering:
    def __init__(self, own, full, lanes, block, sends, arrivals, corner_over_x=()):
        self.own, self.full, self.block, self.sends, self.arrivals = own, full, block, sends, arrivals
        self.corner_over_x, self.lanes = corner_over_x, lanes
        self.started = []

    def place(self, t, dx, dy, dcore=0):
        z, x, y, core = my_place()
        ctx_block = lax.rem(z - t + Z_SIZE, Z_SIZE) * 2 + flipped(x, dx)
        first, second = self.block(ctx_block, flipped(y, dy) * 2 + flipped(core, dcore))
        return self.full.at[first, second, :, self.lanes]

    def copy(self, source, target, number, axis):
        return pltpu.make_async_remote_copy(
            src_ref=source,
            dst_ref=target,
            send_sem=self.sends.at[number],
            recv_sem=self.arrivals.at[number],
            device_id=neighbour(axis),
            device_id_type=pl.DeviceIdType.MESH,
        )

    def send(self, piece, number, axis):
        place = self.place(*piece)
        source = self.own.at[:, self.lanes] if piece == (0, 0, 0) else place
        self.copy(source, place, number, axis).start()
        self.started.append((piece, number))

    def wait(self, piece, number, dcore=0):
        place = self.place(*piece, dcore)
        self.copy(place, place, number, "core").wait_recv()

    def to_core(self, piece):
        t, dx, dy = piece
        self.send(piece, 15 + 4 * t + 2 * dx + dy, "core")

    def over_z(self, t):
        if t < Z_SIZE - 1:
            self.send((t, 0, 0), t, "z")

    def over_plane(self, t):
        self.send((t, 0, 0), 3 + t, "x")
        self.send((t, 0, 0), 7 + t, "y")

    def begin(self):
        self.over_z(0)
        self.over_plane(0)
        self.to_core((0, 0, 0))

    def pass_on(self, t):
        self.wait((t, 0, 0), t - 1)
        self.over_z(t)
        self.over_plane(t)
        self.to_core((t, 0, 0))

    def sides(self, t):
        self.wait((t, 1, 0), 3 + t)
        if t not in self.corner_over_x:
            self.send((t, 1, 0), 11 + t, "y")
        self.to_core((t, 1, 0))
        self.wait((t, 0, 1), 7 + t)
        if t in self.corner_over_x:
            self.send((t, 0, 1), 11 + t, "x")
        self.to_core((t, 0, 1))

    def corner(self, t):
        self.wait((t, 1, 1), 11 + t)
        self.to_core((t, 1, 1))

    def finish(self, t):
        for dx in range(2):
            for dy in range(2):
                self.wait((t, dx, dy), 15 + 4 * t + 2 * dx + dy, 1)

    def drain(self):
        for piece, number in self.started:
            place = self.place(*piece)
            self.copy(place, place, number, "core").wait_send()


class PlaneGathering(Gathering):
    def begin(self):
        self.send((0, 0, 0), 0, "x")
        self.send((0, 0, 0), 1, "y")
        self.to_core((0, 0, 0))

    def plane_sides(self):
        self.wait((0, 1, 0), 0)
        self.send((0, 1, 0), 2, "y")
        self.to_core((0, 1, 0))
        self.wait((0, 0, 1), 1)
        self.to_core((0, 0, 1))

    def plane_corner(self):
        self.wait((0, 1, 1), 2)
        self.to_core((0, 1, 1))

    def ring(self, t):
        for dx in range(2):
            for dy in range(2):
                number = 3 + 4 * t + 2 * dx + dy
                if t:
                    self.wait((t, dx, dy), number - 4)
                if t < Z_SIZE - 1:
                    self.send((t, dx, dy), number, "z")
                if t:
                    self.to_core((t, dx, dy))


def neighbour(axis):
    z, x, y, core = my_place()
    if axis == "z":
        z = lax.rem(z + 1, Z_SIZE)
    elif axis == "z_back":
        z = lax.rem(z + Z_SIZE - 1, Z_SIZE)
    elif axis == "z_two":
        z = lax.rem(z + 2, Z_SIZE)
    elif axis == "x":
        x = 1 - x
    elif axis == "y":
        y = 1 - y
    elif axis == "core":
        core = 1 - core
    elif axis == "y_core":
        y, core = 1 - y, 1 - core
    return (y * 2 + core, z * 2 + x)


def meet(axes):
    barrier = pltpu.get_barrier_semaphore()
    for axis in axes:
        pl.semaphore_signal(barrier, inc=1, device_id=neighbour(axis), device_id_type=pl.DeviceIdType.MESH)
    pl.semaphore_wait(barrier, len(axes))


def front_kernel(
    prefix,
    frequency,
    query_weight,
    key_weight,
    value_weight,
    out_weight,
    gate_weight,
    up_weight,
    down_weight,
    both_gains,
    tokens,
    cotangent,
    qkv_out,
    pairs_out,
    rows_turned,
    both_grads,
    hidden_both,
    attended_both,
    cot_turned,
    proj_turned,
    query_out,
    attended,
    log_total,
    gain_out,
    output,
    mixed_grad,
    attended_grad,
    gain_grad,
    cosine,
    sine,
    limit,
    qkv_own,
    down_own,
    up_own,
    gains_own,
    qkv,
    down,
    up,
    pairs,
    gates,
    ups,
    wide,
    keys,
    values,
    gains,
    rows_two,
    rows_stage,
    hidden,
    attended_rows,
    grads,
    cot_stage,
    proj_stage,
    qkv_sends,
    qkv_arrivals,
    down_sends,
    down_arrivals,
    plane_sends,
    plane_arrivals,
    up_sends,
    up_arrivals,
    pair_sends,
    pair_arrivals,
    gain_sends,
    gain_arrivals,
    own_sems,
    core_sends,
    core_arrivals,
    core_own_sems,
):
    z, x, y, core = my_place()
    seq_at, ctx_at = y * 2 + core, z * 2 + x
    by_ctx, by_seq = (lambda ctx, seq: (ctx, seq)), (lambda ctx, seq: (seq, ctx))
    first = Gathering(qkv_own, qkv, slice(0, 240), by_ctx, qkv_sends, qkv_arrivals, (1, 3))
    plane = PlaneGathering(down_own, down, slice(0, PLANE_LANES), by_seq, plane_sends, plane_arrivals)
    rest = (
        Gathering(down_own, down, slice(PLANE_LANES, 1056), by_seq, down_sends, down_arrivals, (3,)),
        Gathering(up_own, up, slice(0, 768), by_ctx, up_sends, up_arrivals, (3,)),
    )
    mine, theirs, width = core_rows(core), core_rows(1 - core), tokens.shape[1]
    turned = jnp.concatenate([query_weight[...], key_weight[...], value_weight[...]], axis=0)
    qkv_own[...] = turned.astype(F32).T.astype(BF16)
    gains_own[...] = jnp.concatenate([both_gains[...], jnp.zeros((6, 288), F32)], axis=0)
    down_own[:, :768] = down_weight[...]
    down_own[:, 768:] = out_weight[...]
    up_own[:, :384] = gate_weight[...]
    up_own[:, 384:] = up_weight[...]
    meet(("z", "z_back", "x", "y", "core", "y_core"))
    first.begin()
    gain_copies = []
    for number, axis in enumerate(("core", "y", "y_core")):
        copy = pltpu.make_async_remote_copy(
            src_ref=gains_own,
            dst_ref=gains.at[seq_at],
            send_sem=gain_sends.at[number],
            recv_sem=gain_arrivals.at[number],
            device_id=neighbour(axis),
            device_id_type=pl.DeviceIdType.MESH,
        )
        copy.start()
        gain_copies.append(copy)
    own_copies = [
        pltpu.make_async_copy(source, target, own_sems.at[number])
        for number, (source, target) in enumerate(
            (
                (qkv_own, first.place(0, 0, 0)),
                (down_own, down.at[seq_at, ctx_at]),
                (up_own, up.at[ctx_at, seq_at]),
                (gains_own, gains.at[seq_at]),
            )
        )
    ]
    for copy in own_copies:
        copy.start()
    places = ctx_at * 256 + lax.broadcasted_iota(jnp.int32, (256, LANES), 0)
    angles = places.astype(F32) * frequency[...]
    lower = lax.rem(lane_ids(256), HEAD_SIZE) < HEAD_SIZE // 2
    sines = jnp.sin(angles)
    cosine[...] = jnp.cos(angles)
    sine[...] = jnp.where(lower, -sines, sines)
    limit[...] = jnp.maximum(ctx_at * 256 + 1 + lax.broadcasted_iota(jnp.int32, (1, 256), 1), prefix[0])
    for t in range(1, Z_SIZE):
        first.pass_on(t)
        if t == 1:
            plane.begin()
        if t == Z_SIZE - 2:
            for group in rest:
                group.over_z(0)
        first.sides(t - 1)
    plane.plane_sides()
    first.sides(Z_SIZE - 1)
    for group in rest:
        group.over_plane(0)
        group.to_core((0, 0, 0))
    plane.plane_corner()
    plane.ring(0)
    for number, flips in enumerate(((0, 1), (1, 0), (1, 1))):
        place = gains.at[flipped(y, flips[0]) * 2 + flipped(core, flips[1])]
        pltpu.make_async_remote_copy(
            src_ref=place,
            dst_ref=place,
            send_sem=gain_sends.at[number],
            recv_sem=gain_arrivals.at[number],
            device_id=neighbour("core"),
            device_id_type=pl.DeviceIdType.MESH,
        ).wait_recv()
    for copy in own_copies:
        copy.wait()
    for row in range(4):
        gain_out[:, row * 288 : (row + 1) * 288] = gains[row]
    _, hat = normalized(tokens[...].astype(F32))
    rows = (hat * gain_out[0:1, :]).astype(BF16)
    for t in range(Z_SIZE):
        first.corner(t)
    for group in rest:
        group.pass_on(1)
    for t in range(Z_SIZE):
        first.finish(t)

    def multiply(ctx_block, carry):
        matrix = qkv[ctx_block].reshape(tokens.shape[1], 240)
        gates[ctx_block, :, :240] = jnp.dot(rows, matrix, preferred_element_type=F32)
        return carry

    lax.fori_loop(0, 8, multiply, 0)
    save_qkv = pltpu.make_async_copy(qkv, qkv_out, own_sems.at[4])
    save_qkv.start()
    q_part, kv_part = 144, 48
    for at in range(8):
        wide[:, at * q_part : (at + 1) * q_part] = gates[at, :, :q_part]
        wide[:, 1152 + at * kv_part : 1152 + (at + 1) * kv_part] = gates[at, :, q_part : q_part + kv_part]
        wide[:, 1536 + at * kv_part : 1536 + (at + 1) * kv_part] = gates[at, :, q_part + kv_part : 240]
    cos_tile, sin_tile = cosine[...], sine[...]
    for pair in range(3):
        key_tile = wide[:, 1152 + pair * LANES : 1152 + (pair + 1) * LANES]
        pairs[ctx_at, :, 2 * pair * LANES : (2 * pair + 1) * LANES] = rotate_halves(
            key_tile, cos_tile, sin_tile
        ).astype(BF16)
        pairs[ctx_at, :, (2 * pair + 1) * LANES : (2 * pair + 2) * LANES] = wide[
            :, 1536 + pair * LANES : 1536 + (pair + 1) * LANES
        ].astype(BF16)
    natural = [
        rotate_halves(wide[:, at * LANES : (at + 1) * LANES], cos_tile, sin_tile) * HEAD_SIZE**-0.5
        for at in range(9)
    ]
    for at, tile in enumerate(pair_tiles(natural)):
        query_out[at] = tile.astype(BF16)

    pair_copies = []

    def pair_place(t, dx):
        return pairs.at[lax.rem(z - t + Z_SIZE, Z_SIZE) * 2 + flipped(x, dx)]

    def pair_copy(place, number, axis):
        return pltpu.make_async_remote_copy(
            src_ref=place,
            dst_ref=place,
            send_sem=pair_sends.at[number],
            recv_sem=pair_arrivals.at[number],
            device_id=neighbour(axis),
            device_id_type=pl.DeviceIdType.MESH,
        )

    def pair_pass(t):
        if t:
            pair_copy(pair_place(t, 0), t - 1, "z").wait_recv()
        for number, axis in ((t, "z"), (3 + t, "x")):
            if axis == "x" or t < Z_SIZE - 1:
                copy = pair_copy(pair_place(t, 0), number, axis)
                copy.start()
                pair_copies.append(copy)

    def in_rest(step):
        for group in rest:
            step(group)

    pair_pass(0)
    in_rest(lambda group: group.pass_on(2))
    pair_pass(1)
    in_rest(lambda group: group.sides(0))
    pair_pass(2)
    plane.ring(1)
    in_rest(lambda group: group.sides(1))
    pair_pass(3)
    cot_stage[...] = turned_blocks(cotangent[...], 8)
    in_rest(lambda group: group.pass_on(3))
    in_rest(lambda group: group.sides(2))
    for t in range(Z_SIZE):
        pair_copy(pair_place(t, 1), 3 + t, "x").wait_recv()
    save_pairs = pltpu.make_async_copy(pairs, pairs_out, own_sems.at[5])
    save_pairs.start()

    key_ids = lax.broadcasted_iota(jnp.int32, (256, tokens.shape[0]), 0)

    def attend_pair(pair):
        key_lanes = pl.ds(pl.multiple_of(pair * 256, 256), LANES)
        value_lanes = pl.ds(pl.multiple_of(pair * 256 + LANES, LANES), LANES)
        for at in range(8):
            for half in range(2):
                keys[half, at] = masked_pair(pairs[at, :, key_lanes], half, 0.0).astype(BF16)
                values[half, at] = masked_pair(pairs[at, :, value_lanes], half, 1.0).T.astype(BF16)

        def attend_member(member, carry):
            tile = query_out[3 * pair + member]
            parts = []
            for half in range(2):
                top = None
                for at in range(8):
                    part = lax.dot_general(keys[half, at], tile, NT, preferred_element_type=F32)
                    part = jnp.where(key_ids < limit[...] - at * 256, part, -1e30)
                    ups[at, :, :256] = part
                    block_top = jnp.max(part, axis=0, keepdims=True)
                    top = block_top if top is None else jnp.maximum(top, block_top)
                total = jnp.zeros((LANES, tile.shape[0]), F32)
                for at in range(8):
                    weight = jnp.exp(ups[at, :, :256] - top).astype(BF16)
                    total = total + jnp.dot(values[half, at], weight, preferred_element_type=F32)
                norm = total[HEAD_SIZE : HEAD_SIZE + 1] if half == 0 else total[:1]
                log_total[3 * pair + member, half : half + 1, :] = top + jnp.log(norm)
                own = total[:HEAD_SIZE] if half == 0 else total[HEAD_SIZE:]
                parts.append(own / norm)
            attended[3 * pair + member] = jnp.concatenate(parts, axis=0).T.astype(BF16)
            return carry

        lax.fori_loop(0, 3, attend_member, 0)

    started, own_copies = [], []

    def core_copy(source, target, number):
        return pltpu.make_async_remote_copy(
            src_ref=source,
            dst_ref=target,
            send_sem=core_sends.at[number],
            recv_sem=core_arrivals.at[number],
            device_id=neighbour("core"),
            device_id_type=pl.DeviceIdType.MESH,
        )

    def keep(source, target, number):
        copy = pltpu.make_async_copy(source, target, core_own_sems.at[number])
        copy.start()
        own_copies.append(copy)

    def share(source, target, number):
        copy = core_copy(source, target, number)
        copy.start()
        started.append(copy)

    def deal(stage, target_of, number):
        for y_at in range(2):
            keep(stage.at[y_at * 2 + core], target_of(y_at), number + y_at)
            share(stage.at[y_at * 2 + 1 - core], target_of(y_at), number + y_at)

    def attend_and_pass(pair, carry):
        attend_pair(pair)

        @pl.when(pair == 0)
        def _():
            plane.ring(2)
            in_rest(lambda group: group.sides(3))

        @pl.when(pair == 1)
        def _():
            in_rest(lambda group: group.corner(0))
            in_rest(lambda group: group.corner(1))

        return carry

    lax.fori_loop(0, 3, attend_and_pass, 0)
    keep(cot_stage, cot_turned.at[:, :, mine], 1)
    share(cot_stage, cot_turned.at[:, :, mine], 1)
    in_rest(lambda group: group.corner(2))
    for at, tile in enumerate(natural_tiles([attended[at].astype(F32) for at in range(9)])):
        wide[:, at * LANES : (at + 1) * LANES] = tile
    for row in range(4):
        attended_rows[row] = wide[:, row * 288 : (row + 1) * 288].astype(BF16)
    rest[0].corner(3)
    for t in range(Z_SIZE):
        rest[0].finish(t)

    def out_block(row):
        return down[row, :, :, 768:].reshape(width, 288)

    def down_block(row):
        return down[row, :, :, :768].reshape(width, 768)

    def gate_block(block):
        return up[block, :, :, :384].reshape(width, 384)

    def up_block(block):
        return up[block, :, :, 384:].reshape(width, 384)

    mixed_grad[...] = tokens[...].astype(F32)
    for row in range(4):
        mixed_grad[...] += lax.dot_general(attended_rows[row], out_block(row), NT, preferred_element_type=F32)
    rest[1].corner(3)
    plane.ring(3)
    deal(attended_rows, lambda y_at: attended_both.at[y_at, mine], 2)
    factor, hat = normalized(mixed_grad[...])
    gain_row = gain_out[1:2, :]
    rows_two[...] = (hat * gain_row).astype(BF16)
    wide[:, :1152] = hat
    for t in range(Z_SIZE):
        rest[1].finish(t)

        def gate_and_up(dx, carry, t=t):
            block = lax.rem(z - t + Z_SIZE, Z_SIZE) * 2 + lax.rem(x + dx, 2)
            gates[block] = jnp.dot(rows_two[...], gate_block(block), preferred_element_type=F32)
            ups[block] = jnp.dot(rows_two[...], up_block(block), preferred_element_type=F32)
            return carry

        lax.fori_loop(0, 2, gate_and_up, 0)
    rows_stage[...] = turned_blocks(rows_two[...], 4)
    for t in range(Z_SIZE):
        plane.finish(t)
    deal(rows_stage, lambda y_at: rows_turned.at[y_at, :, mine], 4)

    def feed_forward(row, carry):
        back = jnp.dot(cotangent[...], down_block(row), preferred_element_type=F32)
        for side in range(2):
            block = 2 * row + side
            gate, up_part = gates[block], ups[block]
            sigmoid = 1.0 / (1.0 + jnp.exp(-gate))
            active = gate * sigmoid
            hidden[row, :, side * 384 : (side + 1) * 384] = (active * up_part).astype(BF16)
            part = back[:, side * 384 : (side + 1) * 384]
            grads[block, :, :384] = (part * up_part * sigmoid * (1.0 + gate * (1.0 - sigmoid))).astype(BF16)
            grads[block, :, 384:] = (part * active).astype(BF16)
        mixed_grad[...] += lax.dot_general(hidden[row], down_block(row), NT, preferred_element_type=F32)
        return carry

    lax.fori_loop(0, 4, feed_forward, 0)
    output[...] = mixed_grad[...].astype(BF16)
    keep(grads, both_grads.at[:, mine, :], 0)
    share(grads, both_grads.at[:, mine, :], 0)
    deal(hidden, lambda y_at: hidden_both.at[y_at, mine], 6)
    mixed_grad[...] = jnp.zeros_like(mixed_grad)

    def rows_back(block, carry):
        part = lax.dot_general(grads[block, :, :384], gate_block(block), NT, preferred_element_type=F32)
        part = part + lax.dot_general(grads[block, :, 384:], up_block(block), NT, preferred_element_type=F32)
        mixed_grad[...] += part
        return carry

    lax.fori_loop(0, 8, rows_back, 0)
    grad_two, hat = mixed_grad[...], wide[:, :1152]
    gain_grad[...] = jnp.sum(grad_two * hat, axis=0, keepdims=True)
    scaled = grad_two * gain_row
    total = cotangent[...].astype(F32) + factor * (
        scaled - hat * jnp.mean(scaled * hat, axis=-1, keepdims=True)
    )
    mixed_grad[...] = total
    rows_two[...] = total.astype(BF16)
    proj_stage[...] = turned_blocks(rows_two[...], 8)
    for row in range(4):
        wide[:, row * 288 : (row + 1) * 288] = jnp.dot(
            rows_two[...], out_block(row), preferred_element_type=F32
        )
    keep(proj_stage, proj_turned.at[:, :, mine], 8)
    share(proj_stage, proj_turned.at[:, :, mine], 8)
    tiles = pair_tiles([wide[:, at * LANES : (at + 1) * LANES] for at in range(9)])
    for at, tile in enumerate(tiles):
        attended_grad[at] = tile.astype(BF16)
    for group in rest + (first, plane):
        group.drain()
    for copy in pair_copies + gain_copies + started:
        copy.wait_send()
    for copy in own_copies + [save_qkv, save_pairs]:
        copy.wait()
    places = [both_grads.at[:, theirs, :], cot_turned.at[:, :, theirs]]
    places += [attended_both.at[y_at, theirs] for y_at in range(2)]
    places += [rows_turned.at[y_at, :, theirs] for y_at in range(2)]
    places += [hidden_both.at[y_at, theirs] for y_at in range(2)]
    places.append(proj_turned.at[:, :, theirs])
    for number, place in enumerate(places):
        core_copy(place, place, number).wait_recv()


def front(prefix, frequency, weights, gains, tokens, cotangent):
    rows, width = tokens.shape
    dma = pltpu.SemaphoreType.DMA
    shape = jax.ShapeDtypeStruct
    qkv_own, down_own, up_own = (288, 240), (144, 1056), (288, 768)
    return pl.pallas_call(
        front_kernel,
        out_shape=(
            shape((8, 4) + qkv_own, BF16),
            shape((8, rows, 768), BF16),
            shape((2, 288, 2 * rows), BF16),
            shape((8, 2 * rows, 768), BF16),
            shape((2, 2 * rows, 768), BF16),
            shape((2, 2 * rows, 288), BF16),
            shape((8, 144, 2 * rows), BF16),
            shape((8, 144, 2 * rows), BF16),
            shape((9, rows, LANES), BF16),
            shape((9, rows, LANES), BF16),
            shape((9, 2, rows), F32),
            shape((8, width), F32),
            shape((rows, width), BF16),
            shape((rows, width), F32),
            shape((9, rows, LANES), BF16),
            shape((1, width), F32),
            shape((rows, LANES), F32),
            shape((rows, LANES), F32),
            shape((1, rows), jnp.int32),
        ),
        in_specs=[pl.BlockSpec(memory_space=pltpu.SMEM)] + vmem_specs(11),
        out_specs=tuple(any_specs(8) + vmem_specs(11)),
        scratch_shapes=[
            pltpu.VMEM(qkv_own, BF16),
            pltpu.VMEM(down_own, BF16),
            pltpu.VMEM(up_own, BF16),
            pltpu.VMEM((8, 288), F32),
            pltpu.VMEM((8, 4) + qkv_own, BF16),
            pltpu.VMEM((4, 8) + down_own, BF16),
            pltpu.VMEM((8, 4) + up_own, BF16),
            pltpu.VMEM((8, rows, 768), BF16),
            pltpu.VMEM((8, rows, 384), F32),
            pltpu.VMEM((8, rows, 384), F32),
            pltpu.VMEM((rows, 1920), F32),
            pltpu.VMEM((2, 8, 256, LANES), BF16),
            pltpu.VMEM((2, 8, LANES, 256), BF16),
            pltpu.VMEM((4, 8, 288), F32),
            pltpu.VMEM((rows, width), BF16),
            pltpu.VMEM((4, 288, rows), BF16),
            pltpu.VMEM((4, rows, 768), BF16),
            pltpu.VMEM((4, rows, 288), BF16),
            pltpu.VMEM((8, rows, 768), BF16),
            pltpu.VMEM((8, 144, rows), BF16),
            pltpu.VMEM((8, 144, rows), BF16),
        ]
        + [dma((31,))] * 8
        + [dma((7,))] * 2
        + [dma((3,))] * 2
        + [dma((6,))]
        + [dma((9,))] * 3,
        compiler_params=pltpu.CompilerParams(
            vmem_limit_bytes=VMEM_LIMIT, collective_id=1, has_side_effects=True
        ),
        cost_estimate=cost(4 * 18 * rows * 2048 * 128 * 4, 4e8, 18 * rows * 2048),
        name="front",
    )(prefix, frequency, *weights, gains, tokens, cotangent)


class Scattering:
    def __init__(self, buffers, sends, arrivals, out, piece, corners):
        self.corner, self.side_x, self.side_y, self.near_x, self.near_y, self.ring = buffers
        self.sends, self.arrivals, self.out, self.piece, self.corners = sends, arrivals, out, piece, corners

    def copy(self, source, target, number, axis):
        return pltpu.make_async_remote_copy(
            src_ref=source,
            dst_ref=target,
            send_sem=self.sends.at[number],
            recv_sem=self.arrivals.at[number],
            device_id=neighbour(axis),
            device_id_type=pl.DeviceIdType.MESH,
        )

    def corner_copies(self, t, axes=("x", "y")):
        for number, (axis, lanes) in enumerate(self.corners):
            if axis in axes:
                target = self.side_x if axis == "y" else self.side_y
                yield self.copy(self.corner.at[t, :, lanes], target.at[t, :, lanes], 4 * number + t, axis)

    def side_copy(self, t, axis):
        source, target, first = (self.side_x, self.near_x, 8) if axis == "x" else (self.side_y, self.near_y, 12)
        return self.copy(source.at[t], target.at[t], first + t, axis)

    def ring_copy(self, t):
        return self.copy(self.near_x.at[t], self.ring.at[t - 1], 15 + t, "z_back")

    def corner_step(self, t):
        self.piece(t, 1, 1, self.corner.at[t], lambda lanes: [])
        for copy in self.corner_copies(t):
            copy.start()

    def side_step(self, t, axis):
        came = "y" if axis == "x" else "x"
        for copy in self.corner_copies(t, (came,)):
            copy.wait_recv()
        side = (self.side_x if axis == "x" else self.side_y).at[t]
        ranges = [lanes for at, lanes in self.corners if at == came]

        def addend(lanes):
            return [side[:, lanes]] if any(at.start <= lanes.start and lanes.stop <= at.stop for at in ranges) else []

        self.piece(t, int(axis == "x"), int(axis == "y"), side, addend)
        self.side_copy(t, axis).start()

    def near_step(self, t):
        self.side_copy(t, "x").wait_recv()
        self.side_copy(t, "y").wait_recv()
        if t < Z_SIZE - 1:
            self.ring_copy(t + 1).wait_recv()

        def addend(lanes):
            parts = [self.near_x[t, :, lanes], self.near_y[t, :, lanes]]
            return parts + ([self.ring[t, :, lanes]] if t < Z_SIZE - 1 else [])

        self.piece(t, 0, 0, self.near_x.at[t] if t else self.out, addend)
        if t:
            self.ring_copy(t).start()

    def drain(self):
        for t in range(Z_SIZE):
            for copy in self.corner_copies(t):
                copy.wait_send()
            self.side_copy(t, "x").wait_send()
            self.side_copy(t, "y").wait_send()
            if t:
                self.ring_copy(t).wait_send()


class PlaneScattering:
    def __init__(self, buffers, sends, arrivals, out, piece):
        self.sums, self.corner, self.near_x, self.near_y = buffers
        self.sends, self.arrivals, self.out, self.piece = sends, arrivals, out, piece

    def copy(self, source, target, number, axis):
        return pltpu.make_async_remote_copy(
            src_ref=source,
            dst_ref=target,
            send_sem=self.sends.at[number],
            recv_sem=self.arrivals.at[number],
            device_id=neighbour(axis),
            device_id_type=pl.DeviceIdType.MESH,
        )

    def ring_copy(self, t, dx, dy):
        return self.copy(
            self.sums.at[t, dx, dy], self.sums.at[t - 1, dx, dy], 4 * (t - 1) + 2 * dx + dy, "z_back"
        )

    def plane_copies(self):
        return (
            self.copy(self.sums.at[0, 1, 1], self.corner, 12, "y"),
            self.copy(self.sums.at[0, 1, 0], self.near_x, 13, "x"),
            self.copy(self.sums.at[0, 0, 1], self.near_y, 14, "y"),
        )

    def ring_step(self, t, first=False):
        def one(number, carry):
            dx, dy = number // 2, lax.rem(number, 2)
            target = self.sums.at[t, dx, dy]
            if not first:
                self.ring_copy(t + 1, dx, dy).wait_recv()
            self.piece(t, dx, dy, target, lambda lanes: [] if first else [target[:, lanes]])

            @pl.when(t > 0)
            def _():
                self.ring_copy(t, dx, dy).start()

            return carry

        lax.fori_loop(0, 4, one, 0)

    def plane_start(self):
        corner, _, side_y = self.plane_copies()
        corner.start()
        side_y.start()

    def plane_side(self):
        corner, side_x, _ = self.plane_copies()
        corner.wait_recv()
        side = self.sums.at[0, 1, 0]
        side[...] = (side[...].astype(F32) + self.corner[...].astype(F32)).astype(BF16)
        side_x.start()

    def plane_end(self):
        _, side_x, side_y = self.plane_copies()
        side_x.wait_recv()
        side_y.wait_recv()
        total = self.sums[0, 0, 0].astype(F32) + self.near_x[...].astype(F32)
        self.out[...] = total + self.near_y[...].astype(F32)

    def drain(self):
        for t in range(1, Z_SIZE):
            for dx in range(2):
                for dy in range(2):
                    self.ring_copy(t, dx, dy).wait_send()
        for copy in self.plane_copies():
            copy.wait_send()


def back_kernel(
    rows_turned,
    both_grads,
    hidden,
    attended_rows,
    cot_turned,
    proj_turned,
    query,
    attended,
    grad,
    log_total,
    limit,
    cosine,
    sine,
    pairs,
    tokens,
    gains,
    second_gain,
    weights,
    mixed_grad,
    down_out,
    up_out,
    qkv_out,
    input_grad,
    gain_out,
    *refs,
):
    down_buffers, up_buffers, qkv_buffers, plane_buffers = refs[:6], refs[6:12], refs[12:18], refs[18:22]
    (
        keys,
        keys_turned,
        values,
        query_halves,
        grad_halves,
        turned_sum,
        shifts,
        pair_parts,
        pair_near,
        pair_ring,
        query_grad,
        wide,
        pieces,
        first_stage,
        first_turned,
        weight_slots,
        gain_sum,
        gain_came,
    ) = refs[22:40]
    (
        down_sends,
        down_arrivals,
        up_sends,
        up_arrivals,
        qkv_sends,
        qkv_arrivals,
        plane_sends,
        plane_arrivals,
        pair_sends,
        pair_arrivals,
        core_sends,
        core_arrivals,
        gain_sends,
        gain_arrivals,
        own_sems,
        weight_sems,
    ) = refs[40:]
    z, x, y, core = my_place()
    mine, theirs = core_rows(core), core_rows(1 - core)
    rows, width = tokens.shape

    def flip_if(at, flip):
        return flipped(at, flip) if isinstance(flip, int) else lax.rem(at + flip, 2)

    def ctx_of(t, dx):
        return lax.rem(z - t + Z_SIZE, Z_SIZE) * 2 + flip_if(x, dx)

    def put(target, lanes, value, addend):
        for part in addend(lanes):
            value = value + part.astype(F32)
        target[:, lanes] = value.astype(target.dtype)

    def plane_piece(t, dx, dy, target, addend):
        block, row = ctx_of(t, dx), flip_if(y, dy)
        for lanes in (slice(0, 256), slice(256, PLANE_LANES)):
            value = jnp.dot(cot_turned[block], hidden[row, :, lanes], preferred_element_type=F32)
            put(target, lanes, value, addend)

    def down_piece(t, dx, dy, target, addend):
        block, row = ctx_of(t, dx), flipped(y, dy)
        split = 768 - PLANE_LANES
        value = jnp.dot(cot_turned[block], hidden[row, :, PLANE_LANES:], preferred_element_type=F32)
        put(target, slice(0, split), value, addend)
        value = jnp.dot(proj_turned[block], attended_rows[row], preferred_element_type=F32)
        put(target, slice(split, split + 288), value, addend)

    def up_piece(t, dx, dy, target, addend):
        block, row = ctx_of(t, dx), flipped(y, dy)
        for lanes in (slice(0, 384), slice(384, 768)):
            value = jnp.dot(rows_turned[row], both_grads[block, :, lanes], preferred_element_type=F32)
            put(target, lanes, value, addend)

    def qkv_piece(t, dx, dy, target, addend):
        block, row = ctx_of(t, dx), flipped(y, dy)
        value = jnp.dot(first_turned[row], pieces[block], preferred_element_type=F32)
        put(target, slice(0, 240), value, addend)

    plane = PlaneScattering(
        plane_buffers, plane_sends, plane_arrivals, down_out.at[:, :PLANE_LANES], plane_piece
    )
    down = Scattering(
        down_buffers,
        down_sends,
        down_arrivals,
        down_out.at[:, PLANE_LANES:],
        down_piece,
        (("y", slice(0, 1056 - PLANE_LANES)),),
    )
    up = Scattering(
        up_buffers, up_sends, up_arrivals, up_out, up_piece, (("y", slice(0, 384)), ("x", slice(384, 768)))
    )
    qkv = Scattering(qkv_buffers, qkv_sends, qkv_arrivals, qkv_out, qkv_piece, (("y", slice(0, 240)),))

    meet(("z", "z_back", "x", "y", "core", "z_two"))
    residual = pltpu.make_async_copy(mixed_grad, input_grad, own_sems.at[2])
    residual.start()

    plane.ring_step(Z_SIZE - 1, True)

    def corners(number, carry):
        t = Z_SIZE - 1 - number
        down.corner_step(t)
        up.corner_step(t)
        return carry

    lax.fori_loop(0, Z_SIZE, corners, 0)

    factor, hat = normalized(tokens[...].astype(F32))
    first_stage[...] = turned_blocks((hat * gains[0:1, :]).astype(BF16), 4)

    def core_copy(source, target, number):
        return pltpu.make_async_remote_copy(
            src_ref=source,
            dst_ref=target,
            send_sem=core_sends.at[number],
            recv_sem=core_arrivals.at[number],
            device_id=neighbour("core"),
            device_id_type=pl.DeviceIdType.MESH,
        )

    def pair_copy(pair, t, axis):
        if axis == "x":
            source, target, number = pair_parts.at[pair, 1, t], pair_near.at[pair, t], 4 * pair + t
        else:
            source, target, number = pair_parts.at[pair, 0, t], pair_ring.at[pair, t - 1], 11 + 3 * pair + t
        return pltpu.make_async_remote_copy(
            src_ref=source,
            dst_ref=target,
            send_sem=pair_sends.at[number],
            recv_sem=pair_arrivals.at[number],
            device_id=neighbour(axis),
            device_id_type=pl.DeviceIdType.MESH,
        )

    key_ids = lax.broadcasted_iota(jnp.int32, (256, rows), 0)

    def attend_pair_back(pair):
        key_lanes = pl.ds(pl.multiple_of(pair * 256, 256), LANES)
        value_lanes = pl.ds(pl.multiple_of(pair * 256 + LANES, LANES), LANES)
        for at in range(8):
            key_block, value_block = pairs[at, :, key_lanes], pairs[at, :, value_lanes]
            for half in range(2):
                span = slice(256 * half, 256 * (half + 1))
                masked = masked_pair(key_block, half, 0.0)
                keys[at, span] = masked.astype(BF16)
                keys_turned[at, :, span] = masked.T.astype(BF16)
                values[at, span] = masked_pair(value_block, half, 0.0).astype(BF16)
        for member in range(3):
            number = 3 * pair + member
            product = (attended[number].astype(F32) * grad[number].astype(F32)).T
            for half in range(2):
                own = slice(half * HEAD_SIZE, (half + 1) * HEAD_SIZE)
                at = 2 * member + half
                shifts[at] = jnp.sum(product[own], axis=0, keepdims=True)
                query_halves[256 * at : 256 * (at + 1)] = masked_pair(query[number], half, 0.0).astype(BF16)
                grad_halves[256 * at : 256 * (at + 1)] = masked_pair(grad[number], half, 0.0).astype(BF16)
        turned_sum[...] = jnp.zeros_like(turned_sum)

        def block_step(at, carry):
            probs, scores = [], []
            seen = key_ids < limit[...] - at * 256
            for member in range(3):
                number = 3 * pair + member
                parts = lax.dot_general(keys[at], query[number], NT, preferred_element_type=F32)
                backs = lax.dot_general(values[at], grad[number], NT, preferred_element_type=F32)
                for half in range(2):
                    span = slice(256 * half, 256 * (half + 1))
                    part = jnp.where(seen, parts[span], -1e30)
                    prob = jnp.exp(part - log_total[number, half : half + 1, :])
                    scores.append((prob * (backs[span] - shifts[2 * member + half])).astype(BF16))
                    probs.append(prob.astype(BF16))
                turned_sum[member] += jnp.dot(
                    keys_turned[at], jnp.concatenate(scores[-2:], axis=0), preferred_element_type=F32
                )
            t = lax.rem(z - at // 2 + Z_SIZE, Z_SIZE)
            dx = lax.rem(at + x, 2)
            for lanes, left, right in (
                (slice(0, LANES), scores, query_halves),
                (slice(LANES, 2 * LANES), probs, grad_halves),
            ):
                value = jnp.dot(jnp.concatenate(left, axis=1), right[...], preferred_element_type=F32)
                pair_parts[pair, dx, t, :, lanes] = value.astype(BF16)
            return carry

        lax.fori_loop(0, 8, block_step, 0)
        for member in range(3):
            turned = turned_sum[member].T * HEAD_SIZE**-0.5
            query_grad[3 * pair + member] = rotate_halves(turned, cosine[...], -sine[...]).astype(BF16)
        for t in range(Z_SIZE - 1, -1, -1):
            pair_copy(pair, t, "x").start()

    def pair_step(t, pair):
        pair_copy(pair, t, "x").wait_recv()
        total = pair_parts[pair, 0, t].astype(F32) + pair_near[pair, t].astype(F32)
        if t < Z_SIZE - 1:
            pair_copy(pair, t + 1, "z_back").wait_recv()
            total = total + pair_ring[pair, t].astype(F32)
        if t:
            pair_parts[pair, 0, t] = total.astype(BF16)
            pair_copy(pair, t, "z_back").start()
        else:
            key_tile = rotate_halves(total[:, :LANES], cosine[...], -sine[...])
            wide[:, 1152 + pair * LANES : 1152 + (pair + 1) * LANES] = key_tile
            wide[:, 1536 + pair * LANES : 1536 + (pair + 1) * LANES] = total[:, LANES:]

    def side_step(t, axis):
        down.side_step(t, axis)
        up.side_step(t, axis)

    def attend_step(pair, carry):
        attend_pair_back(pair)

        @pl.when(pair == 0)
        def _():
            plane.ring_step(2)
            side_step(3, "y")
            side_step(3, "x")

        @pl.when(pair == 1)
        def _():
            side_step(2, "y")

        return carry

    lax.fori_loop(0, 3, attend_step, 0)
    plane.ring_step(1)
    side_step(2, "x")
    side_step(1, "y")
    first_copies = []
    for y_at in range(2):
        place = first_turned.at[y_at, :, mine]
        own = pltpu.make_async_copy(first_stage.at[y_at * 2 + core], place, own_sems.at[y_at])
        own.start()
        copy = core_copy(first_stage.at[y_at * 2 + 1 - core], place, 1 + y_at)
        copy.start()
        first_copies.append((own, copy))

    for at, tile in enumerate(natural_tiles([query_grad[at].astype(F32) for at in range(9)])):
        wide[:, at * LANES : (at + 1) * LANES] = tile
    q_part, kv_part = 144, 48
    for at in range(8):
        pieces[at, mine, :q_part] = wide[:, at * q_part : (at + 1) * q_part].astype(BF16)
    pair_step(3, 0)
    pair_step(3, 1)
    side_step(1, "x")
    side_step(0, "y")
    side_step(0, "x")
    pair_step(2, 0)
    pair_step(3, 2)
    pair_step(2, 1)
    plane.ring_step(0)
    plane.plane_start()
    pair_step(1, 0)
    pair_step(2, 2)
    pair_step(1, 1)
    pair_step(0, 0)
    pair_step(1, 2)
    down.near_step(3)
    up.near_step(3)
    pair_step(0, 1)
    pair_step(0, 2)
    for at in range(8):
        both = jnp.concatenate(
            [
                wide[:, 1152 + at * kv_part : 1152 + (at + 1) * kv_part],
                wide[:, 1536 + at * kv_part : 1536 + (at + 1) * kv_part],
            ],
            axis=1,
        )
        pieces[at, mine, q_part:] = both.astype(BF16)

    def weight_copy(at):
        return pltpu.make_async_copy(weights.at[at], weight_slots.at[at % 2], weight_sems.at[at % 2])

    weight_copy(0).start()
    weight_copy(1).start()
    piece_copy = core_copy(pieces.at[:, mine, :], pieces.at[:, mine, :], 0)
    piece_copy.start()
    grad_one = wide.at[:, :1152]
    for at in range(8):
        weight_copy(at).wait()
        part = lax.dot_general(
            pieces[at, mine, :], weight_slots[at % 2].reshape(width, 240), NT, preferred_element_type=F32
        )
        grad_one[...] = part if at == 0 else grad_one[...] + part
        if at < 6:
            weight_copy(at + 2).start()
    plane.plane_side()
    core_copy(pieces.at[:, theirs, :], pieces.at[:, theirs, :], 0).wait_recv()
    for y_at, (own, _) in enumerate(first_copies):
        place = first_turned.at[y_at, :, theirs]
        core_copy(place, place, 1 + y_at).wait_recv()
        own.wait()
    def qkv_corners(number, carry):
        qkv.corner_step(Z_SIZE - 1 - number)
        return carry

    lax.fori_loop(0, Z_SIZE, qkv_corners, 0)
    down.near_step(2)
    up.near_step(2)
    def qkv_sides(number, carry):
        for axis in ("y", "x"):
            qkv.side_step(Z_SIZE - 1 - number, axis)
        return carry

    lax.fori_loop(0, Z_SIZE, qkv_sides, 0)
    residual.wait()
    grad_rows = grad_one[...]
    _, hat = normalized(tokens[...].astype(F32))
    first_gain = jnp.sum(grad_rows * hat, axis=0, keepdims=True)
    scaled = grad_rows * gains[0:1, :]
    input_grad[...] += factor * (scaled - hat * jnp.mean(scaled * hat, axis=-1, keepdims=True))
    both = jnp.concatenate([first_gain, second_gain[...], jnp.zeros((6, width), F32)], axis=0)
    for row in range(4):
        gain_sum[0, row] = both[:, row * 288 : (row + 1) * 288]
    gain_copies = []

    def gain_send(source, number, axis):
        copy = pltpu.make_async_remote_copy(
            src_ref=gain_sum.at[source],
            dst_ref=gain_came.at[number],
            send_sem=gain_sends.at[number],
            recv_sem=gain_arrivals.at[number],
            device_id=neighbour(axis),
            device_id_type=pl.DeviceIdType.MESH,
        )
        copy.start()
        gain_copies.append(copy)
        return copy

    plane.plane_end()
    down.near_step(1)
    up.near_step(1)
    gain_send(0, 0, "core").wait_recv()
    gain_sum[0+1] = gain_sum[0] + gain_came[0]
    qkv.near_step(3)
    gain_send(1, 1, "y").wait_recv()
    gain_sum[1+1] = gain_sum[1] + gain_came[1]
    qkv.near_step(2)
    gain_send(2, 2, "x").wait_recv()
    gain_sum[2+1] = gain_sum[2] + gain_came[2]
    qkv.near_step(1)
    ends = [gain_send(3, 3 + number, axis) for number, axis in enumerate(("z", "z_two", "z_back"))]
    down.near_step(0)
    up.near_step(0)
    qkv.near_step(0)
    for copy in ends:
        copy.wait_recv()
    seq_at = y * 2 + core
    gain_out[...] = (gain_sum[3, seq_at] + gain_came[3, seq_at]) + (gain_came[4, seq_at] + gain_came[5, seq_at])
    for group in (down, up, qkv, plane):
        group.drain()
    for pair in range(3):
        for t in range(Z_SIZE):
            pair_copy(pair, t, "x").wait_send()
            if t:
                pair_copy(pair, t, "z_back").wait_send()
    for copy in gain_copies + [piece_copy] + [copy for _, copy in first_copies]:
        copy.wait_send()


def back(weight_inputs, attention_inputs, tokens, gains, second_gain, weights, mixed_grad):
    rows, width = tokens.shape
    dma, arrays = pltpu.SemaphoreType.DMA, []
    for shape in ((144, 1056 - PLANE_LANES), (288, 768), (288, 240)):
        arrays += [pltpu.VMEM((Z_SIZE,) + shape, BF16)] * 5 + [pltpu.VMEM((Z_SIZE - 1,) + shape, BF16)]
    arrays.append(pltpu.VMEM((Z_SIZE, 2, 2, 144, PLANE_LANES), BF16))
    arrays += [pltpu.VMEM((144, PLANE_LANES), BF16)] * 3
    return pl.pallas_call(
        back_kernel,
        out_shape=(
            jax.ShapeDtypeStruct((144, 1056), F32),
            jax.ShapeDtypeStruct((288, 768), F32),
            jax.ShapeDtypeStruct((288, 240), F32),
            jax.ShapeDtypeStruct((rows, width), F32),
            jax.ShapeDtypeStruct((8, 288), F32),
        ),
        in_specs=vmem_specs(17) + any_specs(2),
        out_specs=tuple(vmem_specs(5)),
        scratch_shapes=arrays
        + [
            pltpu.VMEM((8, 512, LANES), BF16),
            pltpu.VMEM((8, LANES, 512), BF16),
            pltpu.VMEM((8, 512, LANES), BF16),
            pltpu.VMEM((6 * rows, LANES), BF16),
            pltpu.VMEM((6 * rows, LANES), BF16),
            pltpu.VMEM((3, LANES, rows), F32),
            pltpu.VMEM((6, 1, rows), F32),
            pltpu.VMEM((3, 2, Z_SIZE, 256, 2 * LANES), BF16),
            pltpu.VMEM((3, Z_SIZE, 256, 2 * LANES), BF16),
            pltpu.VMEM((3, Z_SIZE - 1, 256, 2 * LANES), BF16),
            pltpu.VMEM((9, rows, LANES), BF16),
            pltpu.VMEM((rows, 1920), F32),
            pltpu.VMEM((8, 2 * rows, 240), BF16),
            pltpu.VMEM((4, 288, rows), BF16),
            pltpu.VMEM((2, 288, 2 * rows), BF16),
            pltpu.VMEM((2, 4, 288, 240), BF16),
            pltpu.VMEM((4, 4, 8, 288), F32),
            pltpu.VMEM((6, 4, 8, 288), F32),
        ]
        + [dma((19,))] * 6
        + [dma((15,))] * 2
        + [dma((21,))] * 2
        + [dma((3,))] * 2
        + [dma((6,))] * 2
        + [dma((3,)), dma((2,))],
        compiler_params=pltpu.CompilerParams(
            vmem_limit_bytes=VMEM_LIMIT, collective_id=3, has_side_effects=True
        ),
        cost_estimate=cost(4 * 18 * rows * 2048 * 128 * 10, 4e8, 18 * rows * 2048),
        name="back",
    )(*weight_inputs, *attention_inputs, tokens, gains, second_gain, weights, mixed_grad)


def finish_kernel(output, input_grad, gains, qkv, down, up, *outs):
    turned = qkv[...].T
    outs[0][...] = output[...]
    outs[1][...] = input_grad[...]
    outs[2][...] = gains[...]
    outs[3][...] = turned[:144]
    outs[4][...] = turned[144:192]
    outs[5][...] = turned[192:]
    outs[6][...] = down[:, 768:]
    outs[7][...] = down[:, :768]
    outs[8][...] = up[:, :384]
    outs[9][...] = up[:, 384:]


def finish(*parts):
    rows, width = parts[0].shape
    shapes = ((8, 288), (144, 288), (48, 288), (48, 288), (144, 288), (144, 768), (288, 384), (288, 384))
    return pl.pallas_call(
        finish_kernel,
        out_shape=(jax.ShapeDtypeStruct((rows, width), BF16), jax.ShapeDtypeStruct((rows, width), F32))
        + tuple(jax.ShapeDtypeStruct(shape, F32) for shape in shapes),
        in_specs=vmem_specs(6),
        out_specs=tuple(vmem_specs(10)),
        cost_estimate=cost(1e6, 8e6),
        name="finish",
    )(*parts)


def permuted_device(
    tokens, prefix, gain_one, w_query, w_key, value_weight, w_out, gain_two, w_gate, w_up, w_down, cotangent
):
    tokens, cotangent = tokens[0], cotangent[0]
    half = HEAD_SIZE // 2
    frequency = ROTARY_BASE ** (-jnp.arange(half, dtype=F32) * 2.0 / HEAD_SIZE)
    (
        qkv,
        pairs,
        *weight_inputs,
        query,
        attended,
        log_total,
        gains,
        output,
        mixed_grad,
        attended_grad,
        second_gain,
        cosine,
        sine,
        limit,
    ) = front(
        prefix,
        jnp.tile(frequency, 4)[None, :],
        (w_query.T, w_key.T, value_weight.T, w_out.T, w_gate, w_up, w_down.T),
        jnp.stack([gain_one, gain_two]).astype(F32),
        tokens,
        cotangent,
    )
    grad_down_out, grad_up, grad_qkv, input_grad, gain_grads = back(
        weight_inputs,
        (query, attended, attended_grad, log_total, limit, cosine, sine, pairs),
        tokens,
        gains,
        second_gain,
        qkv,
        mixed_grad,
    )
    output, input_grad, gain_grads, query_t, key_t, value_t, out_t, down_t, gate, up = finish(
        output, input_grad, gain_grads, grad_qkv, grad_down_out, grad_up
    )
    return (
        output[None],
        input_grad[None],
        gain_grads[0],
        query_t.T,
        key_t.T,
        value_t.T,
        out_t.T,
        gain_grads[1],
        gate,
        up,
        down_t.T,
    )


def permute_plan_fits(mesh, tokens):
    return dict(mesh.shape) == {"seq": 4, "ctx": 8} and tokens.shape == (4, 2048, 1152)


def solution(mesh):
    placed = (
        P("seq", "ctx", None),
        P("seq"),
        P("seq"),
        P("seq", "ctx"),
        P("seq", "ctx"),
        P("seq", "ctx"),
        P("seq", "ctx"),
        P("seq"),
        P("seq", "ctx"),
        P("seq", "ctx"),
        P("seq", "ctx"),
        P("seq", "ctx", None),
    )

    def mapped(device_function):
        return jax.shard_map(
            device_function,
            mesh=mesh,
            in_specs=placed,
            out_specs=(
                P("seq", "ctx", None),
                P("seq", "ctx", None),
                P("seq"),
                P("seq", "ctx"),
                P("seq", "ctx"),
                P("seq", "ctx"),
                P("seq", "ctx"),
                P("seq"),
                P("seq", "ctx"),
                P("seq", "ctx"),
                P("seq", "ctx"),
            ),
            check_vma=False,
        )

    def layer(tokens, *rest):
        return mapped(permuted_device if permute_plan_fits(mesh, tokens) else per_device)(tokens, *rest)

    return layer
```

profile of v0, /device:TPU:0, one launch (start us, length us, event | category | flops | bytes accessed | tf_op | source)
XLA Modules:
  0.0 343.7 jit_solution(2266754408436297242)
XLA Ops:
  1.3 0.6 broadcast_in_dim_tile.3.frequency
  1.9 0.7 stack.9
  2.6 0.7 stack.10
  3.3 0.6 maximum_convert_fusion.both_gains
  3.9 175.4 %front.1 = (bf16[8,4,288,240]{3,2,1,0:T(8,128)(2,1)}, bf16[8,256,768]{2,1,0:T(8,128)(2,1)}, bf16[2,288,512]{2,1,0:T(8,128)(2,1)}, bf16[8,512,768]{2,1,0:T(8,128)...) custom-call(s32[1]{0:T(128)S(6)} %copy.23.prefix, ...), custom_call_target="tpu_custom_call" | custom-call | flops 19327352832 | bytes 400000000 | tf_op jit(solution)/shard_map/front/pallas_call | solution.py:1045
  179.3 159.1 %back.1 = (f32[144,1056]{1,0:T(8,128)}, f32[288,768]{1,0:T(8,128)}, f32[288,240]{1,0:T(8,128)}, f32[256,1152]{1,0:T(8,128)}, f32[8,288]{1,0:T(8,128)}) custom-call(bf16[2,288,512]{2,1,0:T(8,128)(2,1)} %get-tuple-element.46.rows_turned, bf16[8,512,768]{2,1,0:T(8,128)(2,1)} %get-tuple-element.47.both_grads, bf16[2,512,768]{2,1,0:T(8,128)(2,1)} %get-tuple-element.48.hidden, ...), custom_call_target="tpu_custom_call" | custom-call | flops 48318382080 | bytes 400000000 | tf_op jit(solution)/shard_map/back/pallas_call | solution.py:1644
  338.3 4.0 %finish.1 = (bf16[256,1152]{1,0:T(8,128)(2,1)}, f32[256,1152]{1,0:T(8,128)}, f32[8,288]{1,0:T(8,128)}, f32[144,288]{1,0:T(8,128)}, f32[48,288]{1,0:T(8,128)}, /*...) custom-call(bf16[256,1152]{1,0:T(8,128)(2,1)} %get-tuple-element.45.o, ...), custom_call_target="tpu_custom_call" | custom-call | flops 1000000 | bytes 8000000 | tf_op jit(solution)/shard_map/finish/pallas_call | solution.py:1707
  342.3 1.4 slice_reduce_fusion
  (2 shorter events, 0.0 us)
where the time goes:
time: 344 us
  Pallas kernels  338 us (98%)
    pallas_call x1, Pallas kernels, front(): pl.pallas_call(front_kernel, out_shape=(shape((8, 4) + qkv_own, BF16), sh...  175 us
    pallas_call x1, Pallas kernels, back(): pl.pallas_call(back_kernel, out_shape=(jax.ShapeDtypeStruct((144, 1056),...  159 us

commit v1 on v0

--- a/solution.py
+++ b/solution.py
@@ -18,7 +18,7 @@
 LANES = 128
 Z_SIZE = 4
 VMEM_LIMIT = 66_000_000
-PLANE_LANES = 640
+PLANE_LANES = 512
 F32 = jnp.float32
 BF16 = jnp.bfloat16
 NT = (((1,), (1,)), ((), ()))

time: 344 us -> 339 us (0.985)
  Pallas kernels: 338 us -> 334 us
where the time goes in v1:
time: 339 us
  Pallas kernels  334 us (99%)
    pallas_call x1, Pallas kernels, front(): pl.pallas_call(front_kernel, out_shape=(shape((8, 4) + qkv_own, BF16), sh...  173 us
    pallas_call x1, Pallas kernels, back(): pl.pallas_call(back_kernel, out_shape=(jax.ShapeDtypeStruct((144, 1056),...  157 us

profile of v1, /device:TPU:0, one launch (start us, length us, event | category | flops | bytes accessed | tf_op | source)
XLA Modules:
  0.0 339.1 jit_solution(17086749671780556519)
XLA Ops:
  1.3 0.6 broadcast_in_dim_tile.3.frequency
  1.9 0.7 stack.9
  2.6 0.7 stack.10
  3.3 0.6 maximum_convert_fusion.both_gains
  3.9 173.2 %front.1 = (bf16[8,4,288,240]{3,2,1,0:T(8,128)(2,1)}, bf16[8,256,768]{2,1,0:T(8,128)(2,1)}, bf16[2,288,512]{2,1,0:T(8,128)(2,1)}, bf16[8,512,768]{2,1,0:T(8,128)...) custom-call(s32[1]{0:T(128)S(6)} %copy.23.prefix, ...), custom_call_target="tpu_custom_call" | custom-call | flops 19327352832 | bytes 400000000 | tf_op jit(solution)/shard_map/front/pallas_call | solution.py:1045
  177.1 156.6 %back.1 = (f32[144,1056]{1,0:T(8,128)}, f32[288,768]{1,0:T(8,128)}, f32[288,240]{1,0:T(8,128)}, f32[256,1152]{1,0:T(8,128)}, f32[8,288]{1,0:T(8,128)}) custom-call(bf16[2,288,512]{2,1,0:T(8,128)(2,1)} %get-tuple-element.46.rows_turned, bf16[8,512,768]{2,1,0:T(8,128)(2,1)} %get-tuple-element.47.both_grads, bf16[2,512,768]{2,1,0:T(8,128)(2,1)} %get-tuple-element.48.hidden, ...), custom_call_target="tpu_custom_call" | custom-call | flops 48318382080 | bytes 400000000 | tf_op jit(solution)/shard_map/back/pallas_call | solution.py:1644
  333.7 4.0 %finish.1 = (bf16[256,1152]{1,0:T(8,128)(2,1)}, f32[256,1152]{1,0:T(8,128)}, f32[8,288]{1,0:T(8,128)}, f32[144,288]{1,0:T(8,128)}, f32[48,288]{1,0:T(8,128)}, /*...) custom-call(bf16[256,1152]{1,0:T(8,128)(2,1)} %get-tuple-element.45.o, ...), custom_call_target="tpu_custom_call" | custom-call | flops 1000000 | bytes 8000000 | tf_op jit(solution)/shard_map/finish/pallas_call | solution.py:1707
  337.7 1.4 slice_reduce_fusion
  (2 shorter events, 0.0 us)
